TPU v7x, 512 devices: a whole 4x4x16 slice. The times are simulated.
512 devices in a mesh: dfa: 32 (over y, x, z_hi), hid: 16 (over z_lo, core).
Axes of the slice: x: 4, y: 4, z: 16 (z_hi: 2, z_lo: 8; z = z_hi * 8 + z_lo), core: 2. Of those that a mesh axis runs over, the one named last changes fastest.
Arguments:
- beta_last: bfloat16 [256, 32, 16, 64], P('dfa', None, 'hid'), may hold values from -6 to 6
- transition: bfloat16 [32, 16, 64, 32768], P(None, 'hid', None, 'dfa'), may hold values from -0.03125 to 0.03125
- emission: bfloat16 [64, 16, 2048], P(None, 'hid'), may hold values from 0.049804688 to 0.59765625
- successor: int32 [256, 8], replicated, may hold values from 0 to 255
- token_set: int32 [256, 8], replicated, may hold values from 0 to 63
Outputs:
- table: bfloat16 [2, 256, 32, 16, 64], P(None, 'dfa', None, 'hid')
All inputs are finite; a program needn't handle non-finite values.
Results may differ from a plain program's by a relative error of at most 0.0056.
Values may be sent and summed in bfloat16 or wider, within the bound.
No kernel may reach another device: no remote copies, remote signals or barrier semaphores. Data moves between devices by JAX's collectives and lax.ppermute only.
A program may use at most 128 MiB of HBM per device.

v0:
```python
import jax
import jax.numpy as jnp
from jax import lax
from jax.sharding import PartitionSpec as P

POS = 2


def edge_mix(full_cols, emission_rows, succ_rows, set_rows):
    width = full_cols.shape[0]
    count = succ_rows.shape[0]
    nsets = emission_rows.shape[0]
    total = jnp.zeros((width, count), jnp.float32)
    for column in range(succ_rows.shape[1]):
        picked = jnp.take(full_cols, succ_rows[:, column], axis=1)
        one_hot = (
            lax.broadcasted_iota(jnp.int32, (nsets, count), 0) == set_rows[:, column][None, :]
        ).astype(jnp.bfloat16)
        weights = lax.dot_general(
            emission_rows, one_hot, (((0,), (0,)), ((), ())), preferred_element_type=jnp.float32
        )
        total = total + weights * picked.astype(jnp.float32)
    return total.astype(jnp.bfloat16)


def local(beta_last, transition, emission, successor, token_set):
    state_count = beta_last.shape[0]
    block_count = beta_last.shape[1]
    cell_count = beta_last.shape[3]
    width = block_count * cell_count
    beta_cols = beta_last.reshape(state_count, width).T
    trans_block = transition.reshape(width, transition.shape[3])
    emission_rows = emission.reshape(emission.shape[0], width)
    results = []
    for position in range(POS):
        full_cols = lax.all_gather(beta_cols, "dfa", axis=1, tiled=True)
        first_row = lax.axis_index("dfa") * state_count
        succ_own = lax.dynamic_slice_in_dim(successor, first_row, state_count, 0)
        set_own = lax.dynamic_slice_in_dim(token_set, first_row, state_count, 0)
        own_cols = edge_mix(full_cols, emission_rows, succ_own, set_own)
        mixed_cols = lax.all_gather(own_cols, "dfa", axis=1, tiled=True)
        summed = lax.psum_scatter(
            lax.dot_general(
                trans_block,
                mixed_cols,
                (((0,), (0,)), ((), ())),
                preferred_element_type=jnp.float32,
            ),
            "hid",
            scatter_dimension=0,
            tiled=True,
        )
        beta_cols = lax.all_to_all(
            summed.astype(jnp.bfloat16), "dfa", split_axis=1, concat_axis=0, tiled=True
        )
        results = [beta_cols.T.reshape(state_count, block_count, 1, cell_count)] + results
    return jnp.stack(results)


def solution(mesh):
    return jax.shard_map(
        local,
        mesh=mesh,
        in_specs=(
            P("dfa", None, "hid", None),
            P(None, "hid", None, "dfa"),
            P(None, "hid", None),
            P(),
            P(),
        ),
        out_specs=P(None, "dfa", None, "hid", None),
        check_vma=False,
    )
```

profile of v0, /device:TPU:2, one launch (start us, length us, event | category | flops | bytes accessed | tf_op | source)
XLA Modules:
  0.0 713.5 jit_solution(4217858540283520598)
XLA Ops:
  6.5 1.6 reshape.29
  8.2 0.8 constant_dynamic-slice_fusion
  10.7 116.1 %all-gather.5.cloned.1.call-done = bf16[2048,256]{0,1:T(8,128)(2,1)} async-done(((bf16[2048,8]{0,1:T(8,128)(2,1)}), bf16[2048,256]{0,1:T(8,128)(2,1)}) %all-gather.5.cloned.1.call-update) | async-done | bytes 1048592 | tf_op jit(solution)/shard_map/all_gather | solution.py:36
  126.7 2.1 gather_fusion.7
  132.9 0.8 add_convert_fusion.1
  133.8 100.9 %all-gather.7.cloned.1.call-done = bf16[2048,256]{0,1:T(8,128)(2,1)} async-done(((bf16[2048,8]{0,1:T(8,128)(2,1)}), bf16[2048,256]{0,1:T(8,128)(2,1)}) %all-gather.7.cloned.1.call-update) | async-done | bytes 1048592 | tf_op jit(solution)/shard_map/all_gather | solution.py:41
  234.7 3.8 convolution_bitcast_fusion.9
  238.4 1.3 copy.20
  239.8 96.3 %reduce-scatter.7.cloned.1.call-done = f32[64,256]{1,0:T(8,128)} async-done(((f32[1024,256]{1,0:T(8,128)}), f32[64,256]{1,0:T(8,128)}) %reduce-scatter.7.cloned.1.call-update) | async-done | bytes 65552
  336.1 0.9 copy.21
  337.2 25.9 %all_to_all.38 = bf16[32,2,256]{2,1,0:T(2,128)(2,1)S(1)} all-to-all(bf16[32,2,256]{2,1,0:T(2,128)(2,1)S(1)} %reshape.211), channel_id=1, replica_groups=mesh['dfa'=32,'hid'=16] {'dfa'}, dimensions={0} | all-to-all | bytes 65536 | tf_op jit(solution)/shard_map/all_to_all | solution.py:53
  363.2 0.7 all_to_all.31
  364.0 104.5 %all-gather.9.cloned.1.call-done = bf16[2048,256]{0,1:T(8,128)(2,1)} async-done(((bf16[2048,8]{0,1:T(8,128)(2,1)}), bf16[2048,256]{0,1:T(8,128)(2,1)}) %all-gather.9.cloned.1.call-update) | async-done | bytes 1048592 | tf_op jit(solution)/shard_map/all_gather | solution.py:36
  468.5 2.1 gather_fusion.15
  474.6 0.8 add_convert_fusion
  475.5 100.9 %all-gather.11.cloned.1.call-done = bf16[2048,256]{0,1:T(8,128)(2,1)} async-done(((bf16[2048,8]{0,1:T(8,128)(2,1)}), bf16[2048,256]{0,1:T(8,128)(2,1)}) %all-gather.11.cloned.1.call-update) | async-done | bytes 1048592 | tf_op jit(solution)/shard_map/all_gather | solution.py:41
  576.3 3.8 convolution_bitcast_fusion.8
  580.1 1.3 copy.22
  581.4 96.5 %reduce-scatter.9.cloned.1.call-done = f32[64,256]{1,0:T(8,128)} async-done(((f32[1024,256]{1,0:T(8,128)}), f32[64,256]{1,0:T(8,128)}) %reduce-scatter.9.cloned.1.call-update) | async-done | bytes 65552
  677.9 0.9 copy.23
  678.9 0.7 reshape.213
  679.6 10.2 %all-to-all-start.1 = ((bf16[32,2,256]{2,1,0:T(2,128)(2,1)}), bf16[32,2,256]{2,1,0:T(2,128)(2,1)S(1)}, u32[]{:S(2)}, u32[]{:S(2)}) async-start(bf16[32,2,256]{2,1,0:T(2,128)(2,1)} %reshape.213), calls=%async_computation.1 | async-start | bytes 65536 | tf_op jit(solution)/shard_map/all_to_all | solution.py:53
  690.0 15.6 %all-to-all-done.1 = bf16[32,2,256]{2,1,0:T(2,128)(2,1)S(1)} async-done(((bf16[32,2,256]{2,1,0:T(2,128)(2,1)}), bf16[32,2,256]{2,1,0:T(2,128)(2,1)S(1)}, u32[]{:S(2)}, u32[]{:S(2)}) %all-to-all-start.1) | async-done | bytes 32800 | tf_op jit(solution)/shard_map/all_to_all | solution.py:53
  706.0 0.7 pad_maximum_fusion
  (63 shorter events, 10.7 us)
Async XLA Ops:
  6.5 2.6 copy-start
  6.5 120.2 %all-gather.5.cloned.1.call-start = ((), (), s32[]{:S(2)}) async-start(), calls=%async_computation.4 | async-start | bytes 1081344 | tf_op jit(solution)/shard_map/all_gather | solution.py:36
  8.2 226.5 %all-gather.7.cloned.1.call-start = ((), (), s32[]{:S(2)}) async-start(), calls=%async_computation.5 | async-start | bytes 1081344 | tf_op jit(solution)/shard_map/all_gather | solution.py:41
  126.7 2.1 copy-start.1
  133.7 202.3 %reduce-scatter.7.cloned.1.call-start = ((), (), s32[]{:S(2)}) async-start(), calls=%async_computation.8 | async-start | bytes 1114112
  239.8 228.7 %all-gather.9.cloned.1.call-start = ((), (), s32[]{:S(2)}) async-start(), calls=%async_computation.6 | async-start | bytes 1081344 | tf_op jit(solution)/shard_map/all_gather | solution.py:36
  364.0 212.3 %all-gather.11.cloned.1.call-start = ((), (), s32[]{:S(2)}) async-start(), calls=%async_computation.7 | async-start | bytes 1081344 | tf_op jit(solution)/shard_map/all_gather | solution.py:41
  468.5 2.1 copy-start.2
  475.4 214.4 %copy-start.3 = (bf16[2048,8]{0,1:T(8,128)(2,1)S(1)}, bf16[2048,8]{0,1:T(8,128)(2,1)}, u32[]{:S(2)}) copy-start(bf16[2048,8]{0,1:T(8,128)(2,1)} %all_to_all.31) | copy-start | bytes 98308
  475.4 202.5 %reduce-scatter.9.cloned.1.call-start = ((), (), s32[]{:S(2)}) async-start(), calls=%async_computation.9 | async-start | bytes 1114112
  679.6 26.0 %all-to-all-start.1 = ((bf16[32,2,256]{2,1,0:T(2,128)(2,1)}), bf16[32,2,256]{2,1,0:T(2,128)(2,1)S(1)}, u32[]{:S(2)}, u32[]{:S(2)}) async-start(bf16[32,2,256]{2,1,0:T(2,128)(2,1)} %reshape.213), calls=%async_computation.1 | async-start | bytes 65536 | tf_op jit(solution)/shard_map/all_to_all | solution.py:53
Sparse Core Ops, SparseCore 0:
  11.6 115.0 all-gather.4
  133.9 100.7 all-gather.6
  239.9 96.1 reduce-scatter.6
  364.1 104.3 all-gather.8
  475.5 100.7 all-gather.10
  581.6 96.2 reduce-scatter.8
where the time goes:
time: 714 us
  waiting for transfers between devices  631 us (88%)
  blocking collectives  25.9 us (4%)
  local copies, waits for them, and re-layouts  21.4 us (3%)
  between operations  13.8 us (2%)
  starting transfers between devices  10.4 us (1%)
  matrix products  9.82 us (1%)
    all_gather x2, waiting for transfers between devices, local(): full_cols = lax.all_gather(beta_cols, 'dfa', axis=1, tiled=True)  221 us
    all_gather x2, waiting for transfers between devices, local(): mixed_cols = lax.all_gather(own_cols, 'dfa', axis=1, tiled=True)  202 us
    unnamed x8, waiting for transfers between devices  193 us
    all_to_all x1, blocking collectives, local(): lax.all_to_all(summed.astype(jnp.bfloat16), 'dfa', split_axis=1, concat_a...  25.9 us
    all_to_all x1, waiting for transfers between devices, local(): lax.all_to_all(summed.astype(jnp.bfloat16), 'dfa', split_axis=1, concat_a...  15.6 us
  transfers between devices with their start and end apart: 7, of which 7 were waited for; matrix products, arithmetic and copies ran while one was open for 0% of the time, Pallas kernels for 0%

commit v1 on v0

--- a/solution.py
+++ b/solution.py
@@ -33,7 +33,9 @@
     emission_rows = emission.reshape(emission.shape[0], width)
     results = []
     for position in range(POS):
-        full_cols = lax.all_gather(beta_cols, "dfa", axis=1, tiled=True)
+        full_cols = jnp.concatenate(
+            lax.all_to_all(jnp.stack([beta_cols] * lax.axis_size("dfa")), "dfa", 0, 0), axis=1
+        )
         first_row = lax.axis_index("dfa") * state_count
         succ_own = lax.dynamic_slice_in_dim(successor, first_row, state_count, 0)
         set_own = lax.dynamic_slice_in_dim(token_set, first_row, state_count, 0)

time: 714 us -> 611 us (0.86)
  waiting for transfers between devices: 631 us -> 469 us
  blocking collectives: 25.9 us -> 66.6 us
  starting transfers between devices: 10.4 us -> 31.3 us
    all_gather x2 -> x0, waiting for transfers between devices: 221 us -> none  [local(): full_cols = lax.all_gather(beta_cols, 'dfa', axis=1, tiled=True)]
    all_to_all x0 -> x1, blocking collectives: none -> 39.4 us  [local(): lax.all_to_all(jnp.stack([beta_cols] * lax.axis_size('dfa')), 'dfa', 0, 0)]
    all_gather x2, waiting for transfers between devices: 202 us -> 232 us  [local(): mixed_cols = lax.all_gather(own_cols, 'dfa', axis=1, tiled=True)]
    all_to_all x0 -> x1, waiting for transfers between devices: none -> 28.2 us  [local(): lax.all_to_all(jnp.stack([beta_cols] * lax.axis_size('dfa')), 'dfa', 0, 0)]
    all_to_all x0 -> x1, starting transfers between devices: none -> 20.9 us  [local(): lax.all_to_all(jnp.stack([beta_cols] * lax.axis_size('dfa')), 'dfa', 0, 0)]
    unnamed x8 -> x6, waiting for transfers between devices: 193 us -> 193 us
  transfers between devices with their start and end apart: 7 -> 6, of which waited for: 7 -> 6; matrix products, arithmetic and copies ran while one was open for 0% -> 0% of each run, Pallas kernels for 0% -> 0%
where the time goes in v1:
time: 611 us; the launch traced here: 610 us
  waiting for transfers between devices  469 us (77%)
  blocking collectives  66.6 us (11%)
  starting transfers between devices  31.3 us (5%)
  local copies, waits for them, and re-layouts  18.4 us (3%)
  between operations  13.4 us (2%)
  matrix products  9.82 us (2%)
    all_gather x2, waiting for transfers between devices, local(): mixed_cols = lax.all_gather(own_cols, 'dfa', axis=1, tiled=True)  232 us
    unnamed x6, waiting for transfers between devices  193 us
    all_to_all x1, blocking collectives, local(): lax.all_to_all(jnp.stack([beta_cols] * lax.axis_size('dfa')), 'dfa', 0, 0)  39.4 us
    all_to_all x1, waiting for transfers between devices, local(): lax.all_to_all(jnp.stack([beta_cols] * lax.axis_size('dfa')), 'dfa', 0, 0)  28.2 us
    all_to_all x1, blocking collectives, local(): lax.all_to_all(summed.astype(jnp.bfloat16), 'dfa', split_axis=1, concat_a...  27.2 us
    all_to_all x1, starting transfers between devices, local(): lax.all_to_all(jnp.stack([beta_cols] * lax.axis_size('dfa')), 'dfa', 0, 0)  20.9 us
    all_to_all x1, waiting for transfers between devices, local(): lax.all_to_all(summed.astype(jnp.bfloat16), 'dfa', split_axis=1, concat_a...  15.6 us
  transfers between devices with their start and end apart: 6, of which 6 were waited for; matrix products, arithmetic and copies ran while one was open for 0% of the time, Pallas kernels for 0%

profile of v1, /device:TPU:2, one launch (start us, length us, event | category | flops | bytes accessed | tf_op | source)
XLA Modules:
  0.0 610.1 jit_solution(3138104969728397075)
XLA Ops:
  6.5 1.0 reshape.46
  7.5 1.1 stack.8
  8.6 20.9 %all-to-all-start = ((bf16[32,2048,8]{1,2,0:T(8,128)(2,1)}), bf16[32,2048,8]{1,2,0:T(8,128)(2,1)S(1)}, u32[]{:S(2)}, u32[]{:S(2)}) async-start(bf16[32,2048,8]{1,2,0:T(8,128)(2,1)} %stack.8), calls=%async_computation | async-start | bytes 2097152 | tf_op jit(solution)/shard_map/all_to_all | solution.py:37
  29.6 0.8 constant_dynamic-slice_fusion
  32.0 28.2 %all-to-all-done = bf16[32,2048,8]{1,2,0:T(8,128)(2,1)S(1)} async-done(((bf16[32,2048,8]{1,2,0:T(8,128)(2,1)}), bf16[32,2048,8]{1,2,0:T(8,128)(2,1)S(1)}, u32[]{:S(2)}, u32[]{:S(2)}) %all-to-all-start) | async-done | bytes 1048608 | tf_op jit(solution)/shard_map/all_to_all | solution.py:37
  61.3 0.6 gather_fusion.2
  64.8 0.8 add_convert_fusion.1
  65.7 130.1 %all-gather.3.cloned.1.call-done = bf16[2048,256]{0,1:T(8,128)(2,1)} async-done(((bf16[2048,8]{0,1:T(8,128)(2,1)}), bf16[2048,256]{0,1:T(8,128)(2,1)}) %all-gather.3.cloned.1.call-update) | async-done | bytes 1048592 | tf_op jit(solution)/shard_map/all_gather | solution.py:43
  195.8 3.8 convolution_bitcast_fusion.9
  199.6 1.3 copy.14
  201.0 96.2 %reduce-scatter.7.cloned.1.call-done = f32[64,256]{1,0:T(8,128)} async-done(((f32[1024,256]{1,0:T(8,128)}), f32[64,256]{1,0:T(8,128)}) %reduce-scatter.7.cloned.1.call-update) | async-done | bytes 65552
  297.2 0.9 copy.15
  298.3 27.2 %all_to_all.45 = bf16[32,2,256]{2,1,0:T(2,128)(2,1)S(1)} all-to-all(bf16[32,2,256]{2,1,0:T(2,128)(2,1)S(1)} %reshape.232), channel_id=1, replica_groups=mesh['dfa'=32,'hid'=16] {'dfa'}, dimensions={0} | all-to-all | bytes 65536 | tf_op jit(solution)/shard_map/all_to_all | solution.py:55
  325.9 39.4 %all_to_all.46 = bf16[32,2048,8]{1,2,0:T(8,128)(2,1)S(1)} all-to-all(bf16[32,2048,8]{1,2,0:T(8,128)(2,1)S(1)} %stack.10), channel_id=1, replica_groups=mesh['dfa'=32,'hid'=16] {'dfa'}, dimensions={0} | all-to-all | bytes 2097152 | tf_op jit(solution)/shard_map/all_to_all | solution.py:37
  370.0 0.8 add_convert_fusion
  370.8 102.4 %all-gather.5.cloned.1.call-done = bf16[2048,256]{0,1:T(8,128)(2,1)} async-done(((bf16[2048,8]{0,1:T(8,128)(2,1)}), bf16[2048,256]{0,1:T(8,128)(2,1)}) %all-gather.5.cloned.1.call-update) | async-done | bytes 1048592 | tf_op jit(solution)/shard_map/all_gather | solution.py:43
  473.2 3.8 convolution_bitcast_fusion.8
  477.0 1.3 copy.16
  478.3 96.5 %reduce-scatter.9.cloned.1.call-done = f32[64,256]{1,0:T(8,128)} async-done(((f32[1024,256]{1,0:T(8,128)}), f32[64,256]{1,0:T(8,128)}) %reduce-scatter.9.cloned.1.call-update) | async-done | bytes 65552
  574.8 0.9 copy.17
  575.7 0.7 reshape.234
  576.5 10.2 %all-to-all-start.3 = ((bf16[32,2,256]{2,1,0:T(2,128)(2,1)}), bf16[32,2,256]{2,1,0:T(2,128)(2,1)S(1)}, u32[]{:S(2)}, u32[]{:S(2)}) async-start(bf16[32,2,256]{2,1,0:T(2,128)(2,1)} %reshape.234), calls=%async_computation.3 | async-start | bytes 65536 | tf_op jit(solution)/shard_map/all_to_all | solution.py:55
  586.8 15.6 %all-to-all-done.3 = bf16[32,2,256]{2,1,0:T(2,128)(2,1)S(1)} async-done(((bf16[32,2,256]{2,1,0:T(2,128)(2,1)}), bf16[32,2,256]{2,1,0:T(2,128)(2,1)S(1)}, u32[]{:S(2)}, u32[]{:S(2)}) %all-to-all-start.3) | async-done | bytes 32800 | tf_op jit(solution)/shard_map/all_to_all | solution.py:55
  602.9 0.7 pad_maximum_fusion
  (56 shorter events, 11.4 us)
Async XLA Ops:
  6.5 24.0 %copy-start = (bf16[64,1,2048]{2,0,1:T(8,128)(2,1)S(1)}, bf16[64,1,2048]{2,0,1:T(8,128)(2,1)}, u32[]{:S(2)}) copy-start(bf16[64,1,2048]{2,0,1:T(8,128)(2,1)} %param.9) | copy-start | bytes 786436
  8.6 51.5 %all-to-all-start = ((bf16[32,2048,8]{1,2,0:T(8,128)(2,1)}), bf16[32,2048,8]{1,2,0:T(8,128)(2,1)S(1)}, u32[]{:S(2)}, u32[]{:S(2)}) async-start(bf16[32,2048,8]{1,2,0:T(8,128)(2,1)} %stack.8), calls=%async_computation | async-start | bytes 2097152 | tf_op jit(solution)/shard_map/all_to_all | solution.py:37
  29.5 166.3 %all-gather.3.cloned.1.call-start = ((), (), s32[]{:S(2)}) async-start(), calls=%async_computation.6 | async-start | bytes 1081344 | tf_op jit(solution)/shard_map/all_gather | solution.py:43
  65.7 231.5 %reduce-scatter.7.cloned.1.call-start = ((), (), s32[]{:S(2)}) async-start(), calls=%async_computation.8 | async-start | bytes 1114112
  200.9 272.3 %all-gather.5.cloned.1.call-start = ((), (), s32[]{:S(2)}) async-start(), calls=%async_computation.7 | async-start | bytes 1081344 | tf_op jit(solution)/shard_map/all_gather | solution.py:43
  370.8 204.0 %reduce-scatter.9.cloned.1.call-start = ((), (), s32[]{:S(2)}) async-start(), calls=%async_computation.9 | async-start | bytes 1114112
  576.5 26.0 %all-to-all-start.3 = ((bf16[32,2,256]{2,1,0:T(2,128)(2,1)}), bf16[32,2,256]{2,1,0:T(2,128)(2,1)S(1)}, u32[]{:S(2)}, u32[]{:S(2)}) async-start(bf16[32,2,256]{2,1,0:T(2,128)(2,1)} %reshape.234), calls=%async_computation.3 | async-start | bytes 65536 | tf_op jit(solution)/shard_map/all_to_all | solution.py:55
Sparse Core Ops, SparseCore 0:
  65.8 129.9 all-gather.2
  201.0 96.1 reduce-scatter.6
  370.9 102.2 all-gather.4
  478.4 96.2 reduce-scatter.8
